TPU v7x, 512 devices: a whole 4x8x8 slice. The times are simulated.
512 devices in a mesh: dp: 64 (over z, x, core), expert: 8 (over y).
Axes of the slice: x: 4, y: 8, z: 8, core: 2. Of those that a mesh axis runs over, the one named last changes fastest.
Arguments:
- tokens: bfloat16 [512, 4096], P('expert', 'dp'), may hold values from -6 to 6
- cotangent: bfloat16 [512, 4096], P('expert', 'dp'), may hold values from -6 to 6
- gate_logit: float32 [512], P('expert'), may hold values from -8 to 8
- routes: int32 [512, 2], P('expert'), may hold values from 0 to 7, all different within a row; in each aligned block of 64 rows (0 to 63, 64 to 127, ...) at most 32 rows name the same one
- w_up: bfloat16 [8, 14336, 4096], P('expert', 'dp'), may hold values from -0.09375 to 0.09375
- w_down: bfloat16 [8, 14336, 4096], P('expert', 'dp'), may hold values from -0.046875 to 0.046875
- basis: bfloat16 [4096, 256], P('dp'), may hold values from -0.09375 to 0.09375
- sketch: float32 [8, 256, 256], P('expert'), may hold values from -1 to 10, as said below
Outputs:
- token_grad: bfloat16 [512, 4096], P('expert', 'dp')
- sketch_next: float32 [8, 256, 256], P('expert')
- precond: float32 [8, 14336, 256], P('expert', 'dp')
Inputs may be any that keep to these rules, and one draw needn't show every extreme that they name: `routes`: each row names 2 different experts. Among the 64 tokens of one index of expert at most 32 name the same expert, and in some index that many do. `sketch`: each matrix is symmetric, and in every row its diagonal entry exceeds the sum of the magnitudes off the diagonal.
All inputs are finite; a program needn't handle non-finite values.
Results may differ from a plain program's by a relative error of at most 0.0064.
Values may be sent and summed in bfloat16 or wider, within the bound.
A program may use at most 128 MiB of HBM per device.

v0:
```python
import jax
import jax.numpy as jnp
from jax import lax
from jax.sharding import PartitionSpec as P

decay_rate = 0.9
damping = 1.0
highest = lax.Precision.HIGHEST


def per_device(tokens, cotangent, gate_logit, routes, w_up, w_down, basis, sketch):
    experts = lax.axis_size("expert")
    tok_rows = tokens.shape[0]
    width_local = tokens.shape[1]
    capacity = min(tok_rows, tok_rows * 4 // experts)
    slot_count = experts * capacity
    gate_first = jax.nn.sigmoid(gate_logit)
    gates = jnp.stack([gate_first, 1.0 - gate_first], axis=1)
    expert_ids = jnp.arange(experts, dtype=jnp.int32)
    chosen = routes[:, :, None] == expert_ids[None, None, :]
    hit_count = jnp.sum(chosen.astype(jnp.int32), axis=1)
    gate_by_expert = jnp.sum(chosen.astype(jnp.float32) * gates[:, :, None], axis=1)
    before = jnp.cumsum(hit_count, axis=0) - hit_count
    slot_of = expert_ids[None, :] * capacity + before
    slot_ids = jnp.arange(slot_count, dtype=jnp.int32)
    slot_match = (
        (slot_of[None, :, :] == slot_ids[:, None, None]) & (hit_count[None, :, :] > 0)
    ).astype(jnp.float32)
    table = jnp.sum(slot_match, axis=2)
    gate_slot = jnp.sum(slot_match * gate_by_expert[None, :, :], axis=(1, 2))
    table_b = table.astype(jnp.bfloat16)
    x_send = jnp.dot(table_b, tokens, preferred_element_type=jnp.float32).astype(jnp.bfloat16)
    cot_rows = jnp.dot(table_b, cotangent, preferred_element_type=jnp.float32)
    dy_send = (gate_slot[:, None] * cot_rows).astype(jnp.bfloat16)
    x_send = x_send.reshape(experts, capacity, width_local)
    dy_send = dy_send.reshape(experts, capacity, width_local)
    x_recv, dy_recv = (
        lax.all_to_all(x_send, "expert", split_axis=0, concat_axis=0, tiled=True),
        lax.all_to_all(dy_send, "expert", split_axis=0, concat_axis=0, tiled=True),
    )
    x_full, dy_full = (
        lax.all_gather(x_recv, "dp", axis=2, tiled=True),
        lax.all_gather(dy_recv, "dp", axis=2, tiled=True),
    )
    row_block = x_full.reshape(slot_count, -1)
    dy_block = dy_full.reshape(slot_count, -1)
    up_local = w_up[0]
    down_local = w_down[0]
    hidden = lax.dot_general(
        row_block, up_local, (((1,), (1,)), ((), ())), preferred_element_type=jnp.float32
    )
    back_grad = lax.dot_general(
        dy_block, down_local, (((1,), (1,)), ((), ())), preferred_element_type=jnp.float32
    )
    sigma_val = jax.nn.sigmoid(hidden)
    hidden_grad = (back_grad * sigma_val * (1.0 + hidden * (1.0 - sigma_val))).astype(jnp.bfloat16)
    partial_value = jnp.dot(hidden_grad, up_local, preferred_element_type=jnp.float32)
    summed = lax.psum_scatter(partial_value, "dp", scatter_dimension=1, tiled=True).astype(
        jnp.bfloat16
    )
    returned = lax.all_to_all(
        summed.reshape(experts, capacity, width_local),
        "expert",
        split_axis=0,
        concat_axis=0,
        tiled=True,
    )
    token_grad = lax.dot_general(
        table_b,
        returned.reshape(slot_count, width_local),
        (((0,), (0,)), ((), ())),
        preferred_element_type=jnp.float32,
    ).astype(jnp.bfloat16)
    basis_full = lax.all_gather(basis, "dp", axis=0, tiled=True)
    projected = jnp.dot(row_block, basis_full, preferred_element_type=jnp.float32).astype(
        jnp.bfloat16
    )
    coefficients = lax.dot_general(
        projected, hidden_grad, (((0,), (0,)), ((), ())), preferred_element_type=jnp.float32
    )
    gram_part = jnp.dot(coefficients, coefficients.T, precision=highest)
    total_hidden = w_up.shape[1] * lax.axis_size("dp")
    gram_total = lax.psum(gram_part, "dp") / total_hidden
    merged = decay_rate * sketch[0] + gram_total
    factor = jnp.linalg.cholesky(merged + damping * jnp.eye(merged.shape[0], dtype=jnp.float32))
    solved = damping * jax.scipy.linalg.cho_solve((factor, True), coefficients)
    return (token_grad, merged[None], solved.T[None])


def solution(mesh):
    in_specs = (
        P("expert", "dp"),
        P("expert", "dp"),
        P("expert"),
        P("expert", None),
        P("expert", "dp", None),
        P("expert", "dp", None),
        P("dp", None),
        P("expert", None, None),
    )
    out_specs = (P("expert", "dp"), P("expert", None, None), P("expert", "dp", None))
    return jax.shard_map(
        per_device, mesh=mesh, in_specs=in_specs, out_specs=out_specs, check_vma=False
    )
```

profile of v0, /device:TPU:2, one launch (start us, length us, event | category | flops | bytes accessed | tf_op | source)
XLA Modules:
  0.0 657.5 jit_solution(2081533431602891325)
XLA Ops:
  7.2 0.8 convert_reduce_fusion.1
  10.1 0.9 fusion.16
  11.3 14.9 %all_to_all.15 = bf16[8,2,1024]{2,1,0:T(2,128)(2,1)S(1)} all-to-all(bf16[8,2,1024]{2,1,0:T(2,128)(2,1)S(1)} %reshape.113), channel_id=1, replica_groups=mesh['dp'=64,'expert'=8] {'expert'}, dimensions={0} | all-to-all | bytes 65536 | tf_op jit(solution)/shard_map/all_to_all | solution.py:39
  26.3 0.8 copy.44
  27.2 0.9 convolution_convert_fusion.1
  28.3 10.4 %all_to_all.16 = bf16[8,2,1024]{2,1,0:T(2,128)(2,1)S(1)} all-to-all(bf16[8,2,1024]{2,1,0:T(2,128)(2,1)S(1)} %reshape.115), channel_id=1, replica_groups=mesh['dp'=64,'expert'=8] {'expert'}, dimensions={0} | all-to-all | bytes 65536 | tf_op jit(solution)/shard_map/all_to_all | solution.py:38
  38.9 0.8 copy.47
  40.5 74.2 %all-gather.4.cloned.1.call-done = bf16[8,32,4096]{1,0,2:T(8,128)(2,1)} async-done(((bf16[8,32,64]{1,0,2:T(8,128)(2,1)}), bf16[8,32,4096]{1,0,2:T(8,128)(2,1)}) %all-gather.4.cloned.1.call-update) | async-done | bytes 2097168 | tf_op jit(solution)/shard_map/all_gather | solution.py:43
  114.7 9.3 %copy.45 = bf16[8,32,4096]{2,1,0:T(8,128)(2,1)} copy(bf16[8,32,4096]{1,0,2:T(8,128)(2,1)} %all-gather.4.cloned.1.call-done) | data formatting | bytes 4194304 | tf_op jit(solution)/shard_map/all_gather | solution.py:43
  124.0 80.1 %all-gather.6.cloned.1.call-done = bf16[8,32,4096]{1,0,2:T(8,128)(2,1)} async-done(((bf16[8,32,64]{1,0,2:T(8,128)(2,1)}), bf16[8,32,4096]{1,0,2:T(8,128)(2,1)}) %all-gather.6.cloned.1.call-update) | async-done | bytes 2097168 | tf_op jit(solution)/shard_map/all_gather | solution.py:42
  204.1 9.4 %copy.48 = bf16[8,32,4096]{2,1,0:T(8,128)(2,1)} copy(bf16[8,32,4096]{1,0,2:T(8,128)(2,1)} %all-gather.6.cloned.1.call-done) | data formatting | bytes 4194304 | tf_op jit(solution)/shard_map/all_gather | solution.py:42
  213.5 2.5 fusion.2
  216.3 0.8 fusion.12
  217.1 70.8 %all-gather.8.cloned.1.call-done = bf16[4096,256]{1,0:T(8,128)(2,1)} async-done(((bf16[64,256]{1,0:T(8,128)(2,1)}), bf16[4096,256]{1,0:T(8,128)(2,1)}) %all-gather.8.cloned.1.call-update) | async-done | bytes 2097168 | tf_op jit(solution)/shard_map/all_gather | solution.py:74
  287.8 3.1 fusion.15
  291.0 1.3 fusion.34
  292.6 2.9 fusion
  295.5 0.9 copy-done.2
  296.6 181.5 %all-reduce.3.cloned.1.call-done = f32[256,256]{0,1:T(8,128)} async-done(((f32[256,256]{0,1:T(8,128)}), f32[256,256]{0,1:T(8,128)}) %all-reduce.3.cloned.1.call-update) | async-done | bytes 262160 | tf_op jit(solution)/shard_map/psum | solution.py:83
  478.1 1.0 convert_add_fusion
  479.3 11.7 %cholesky.50 = f32[128,128]{1,0:T(8,128)S(1)} custom-call(f32[128,128]{1,0:T(8,128)S(1)} %cholesky.118), custom_call_target="Cholesky" | custom-call | tf_op jit(solution)/shard_map/jit(cholesky)/cholesky | solution.py:85
  491.0 9.8 %custom-call.18 = f32[1,128,128]{1,2,0:T(8,128)S(1)} custom-call(f32[1,128,128]{2,1,0:T(8,128)S(1)} %get-tuple-element.42), custom_call_target="InvertDiagBlocksLowerTriangular" | custom-call | tf_op jit(solution)/shard_map/jit(cholesky)/cholesky | solution.py:85
  501.3 11.7 %cholesky.105 = f32[128,128]{1,0:T(8,128)S(1)} custom-call(f32[128,128]{1,0:T(8,128)S(1)} %convolution_subtract_fusion.2), custom_call_target="Cholesky" | custom-call | tf_op jit(solution)/shard_map/jit(cholesky)/cholesky | solution.py:85
  515.1 4.2 while.1
  515.9 1.4 bitcast_dynamic-update-slice_fusion.2
  517.9 1.4 bitcast_dynamic-update-slice_fusion.2
  519.3 19.7 %custom-call.19 = f32[2,128,128]{1,2,0:T(8,128)S(1)} custom-call(f32[2,128,128]{2,1,0:T(8,128)S(1)} %get-tuple-element.10), custom_call_target="InvertDiagBlocksLowerTriangular" | custom-call | tf_op jit(solution)/shard_map/jit(_cho_solve)/triangular_solve | solution.py:86
  540.6 93.1 %reduce-scatter.2.cloned.1.call-done = f32[256,64]{0,1:T(8,128)} async-done(((f32[256,4096]{0,1:T(8,128)}), f32[256,64]{0,1:T(8,128)}) %reduce-scatter.2.cloned.1.call-update) | async-done | bytes 65552 | tf_op jit(solution)/shard_map/reduce_scatter | solution.py:58
  633.7 0.8 convert_element_type.37
  635.4 6.7 %all-to-all-start.2 = ((bf16[8,2,1024]{2,1,0:T(2,128)(2,1)}), bf16[8,2,1024]{2,1,0:T(2,128)(2,1)S(1)}, u32[]{:S(2)}, u32[]{:S(2)}) async-start(bf16[8,2,1024]{2,1,0:T(2,128)(2,1)} %reshape.117), calls=%async_computation.3 | async-start | bytes 65536 | tf_op jit(solution)/shard_map/all_to_all | solution.py:61
  642.8 0.8 copy.53
  643.7 6.5 all-to-all-done.2
  (63 shorter events, 10.8 us)
Async XLA Ops:
  7.2 206.4 %copy-start = (bf16[1,224,4096]{2,1,0:T(8,128)(2,1)S(1)}, bf16[1,224,4096]{2,1,0:T(8,128)(2,1)}, u32[]{:S(2)}) copy-start(bf16[1,224,4096]{2,1,0:T(8,128)(2,1)} %param.12) | copy-start | bytes 5505028
  7.2 107.5 %all-gather.4.cloned.1.call-start = ((), (), s32[]{:S(2)}) async-start(), calls=%async_computation.4 | async-start | bytes 8519680 | tf_op jit(solution)/shard_map/all_gather | solution.py:43
  27.1 177.0 %all-gather.6.cloned.1.call-start = ((), (), s32[]{:S(2)}) async-start(), calls=%async_computation.5 | async-start | bytes 8519680 | tf_op jit(solution)/shard_map/all_gather | solution.py:42
  39.7 248.2 %all-gather.8.cloned.1.call-start = ((), (), s32[]{:S(2)}) async-start(), calls=%async_computation.7 | async-start | bytes 2129920 | tf_op jit(solution)/shard_map/all_gather | solution.py:74
  40.4 437.7 %all-reduce.3.cloned.1.call-start = ((), (), s32[]{:S(2)}) async-start(), calls=%async_computation.8 | async-start | bytes 524288 | tf_op jit(solution)/shard_map/psum | solution.py:83
  213.5 2.6 copy-start.1
  213.5 2.8 copy-start.3
  292.4 341.3 %reduce-scatter.2.cloned.1.call-start = ((), (), s32[]{:S(2)}) async-start(), calls=%async_computation.6 | async-start | bytes 4259840 | tf_op jit(solution)/shard_map/reduce_scatter | solution.py:58
  295.5 0.9 copy-start.2
  635.4 14.8 %all-to-all-start.2 = ((bf16[8,2,1024]{2,1,0:T(2,128)(2,1)}), bf16[8,2,1024]{2,1,0:T(2,128)(2,1)S(1)}, u32[]{:S(2)}, u32[]{:S(2)}) async-start(bf16[8,2,1024]{2,1,0:T(2,128)(2,1)} %reshape.117), calls=%async_computation.3 | async-start | bytes 65536 | tf_op jit(solution)/shard_map/all_to_all | solution.py:61
Sparse Core Ops, SparseCore 0:
  27.3 87.3 all-gather.3
  118.6 85.4 all-gather.5
  207.5 80.3 all-gather.7
  292.5 185.5 all-reduce.2
  482.6 151.0 reduce-scatter.1
where the time goes:
time: 658 us
  waiting for transfers between devices  507 us (77%)
  other arithmetic  58.9 us (9%)
  local copies, waits for them, and re-layouts  28.5 us (4%)
  blocking collectives  25.3 us (4%)
  matrix products  15.3 us (2%)
  between operations  15.3 us (2%)
  starting transfers between devices  7.12 us (1%)
    psum x1, waiting for transfers between devices, per_device(): gram_total = lax.psum(gram_part, 'dp') / total_hidden  181 us
    reduce_scatter x1, waiting for transfers between devices, per_device(): lax.psum_scatter(partial_value, 'dp', scatter_dimension=1, tiled=True)  93.1 us
    all_gather x1, waiting for transfers between devices, per_device(): lax.all_gather(x_recv, 'dp', axis=2, tiled=True)  80.1 us
    all_gather x1, waiting for transfers between devices, per_device(): lax.all_gather(dy_recv, 'dp', axis=2, tiled=True)  74.2 us
    all_gather x1, waiting for transfers between devices, per_device(): basis_full = lax.all_gather(basis, 'dp', axis=0, tiled=True)  70.8 us
    another operation x6, other arithmetic, per_device(): jnp.linalg.cholesky(merged + damping * jnp.eye(merged.shape[0], dtype=jnp...  34 us
    another operation x3, other arithmetic, per_device(): solved = damping * jax.scipy.linalg.cho_solve((factor, True), coefficients)  19.7 us
    all_to_all x1, blocking collectives, per_device(): lax.all_to_all(dy_send, 'expert', split_axis=0, concat_axis=0, tiled=True)  14.9 us
  transfers between devices with their start and end apart: 6, of which 6 were waited for; matrix products, arithmetic and copies ran while one was open for 14% of the time, Pallas kernels for 0%

commit v1 on v0

--- a/solution.py
+++ b/solution.py
@@ -80,7 +80,7 @@
     )
     gram_part = jnp.dot(coefficients, coefficients.T, precision=highest)
     total_hidden = w_up.shape[1] * lax.axis_size("dp")
-    gram_total = lax.psum(gram_part, "dp") / total_hidden
+    gram_total = jnp.sum(lax.all_gather(gram_part, "dp"), axis=0) / total_hidden
     merged = decay_rate * sketch[0] + gram_total
     factor = jnp.linalg.cholesky(merged + damping * jnp.eye(merged.shape[0], dtype=jnp.float32))
     solved = damping * jax.scipy.linalg.cho_solve((factor, True), coefficients)

time: 658 us -> 630 us (0.957)
  the two profiles are of different devices: /device:TPU:2 before, /device:TPU:1 now
where the time goes in v1:
time: 630 us; the launch traced here: 629 us
  waiting for transfers between devices  475 us (75%)
  other arithmetic  65.1 us (10%)
  local copies, waits for them, and re-layouts  27.9 us (4%)
  blocking collectives  23.6 us (4%)
  between operations  15.4 us (2%)
  matrix products  15.3 us (2%)
  starting transfers between devices  6.66 us (1%)
    reduce_scatter x1, waiting for transfers between devices, per_device(): lax.psum_scatter(partial_value, 'dp', scatter_dimension=1, tiled=True)  145 us
    all_gather x1, waiting for transfers between devices, per_device(): gram_total = jnp.sum(lax.all_gather(gram_part, 'dp'), axis=0) / total_hidden  96.9 us
    all_gather x1, waiting for transfers between devices, per_device(): lax.all_gather(x_recv, 'dp', axis=2, tiled=True)  80 us
    all_gather x1, waiting for transfers between devices, per_device(): lax.all_gather(dy_recv, 'dp', axis=2, tiled=True)  78.5 us
    all_gather x1, waiting for transfers between devices, per_device(): basis_full = lax.all_gather(basis, 'dp', axis=0, tiled=True)  67.5 us
    another operation x6, other arithmetic, per_device(): jnp.linalg.cholesky(merged + damping * jnp.eye(merged.shape[0], dtype=jnp...  34 us
    another operation x3, other arithmetic, per_device(): solved = damping * jax.scipy.linalg.cho_solve((factor, True), coefficients)  19.9 us
    all_to_all x1, blocking collectives, per_device(): lax.all_to_all(dy_send, 'expert', split_axis=0, concat_axis=0, tiled=True)  14.3 us
  transfers between devices with their start and end apart: 6, of which 6 were waited for; matrix products, arithmetic and copies ran while one was open for 5% of the time, Pallas kernels for 0%

profile of v1, /device:TPU:1, one launch (start us, length us, event | category | flops | bytes accessed | tf_op | source)
XLA Modules:
  0.0 629.0 jit_solution(15920578633638807088)
XLA Ops:
  7.2 0.8 convert_reduce_fusion.1
  10.1 0.9 fusion.16
  11.3 14.3 %all_to_all.15 = bf16[8,2,1024]{2,1,0:T(2,128)(2,1)S(1)} all-to-all(bf16[8,2,1024]{2,1,0:T(2,128)(2,1)S(1)} %reshape.123), channel_id=1, replica_groups=mesh['dp'=64,'expert'=8] {'expert'}, dimensions={0} | all-to-all | bytes 65536 | tf_op jit(solution)/shard_map/all_to_all | solution.py:39
  25.7 0.8 copy.42
  26.6 0.9 convolution_convert_fusion.1
  27.7 9.2 %all_to_all.16 = bf16[8,2,1024]{2,1,0:T(2,128)(2,1)S(1)} all-to-all(bf16[8,2,1024]{2,1,0:T(2,128)(2,1)S(1)} %reshape.125), channel_id=1, replica_groups=mesh['dp'=64,'expert'=8] {'expert'}, dimensions={0} | all-to-all | bytes 65536 | tf_op jit(solution)/shard_map/all_to_all | solution.py:38
  37.1 0.8 copy.45
  38.7 78.5 %all-gather.6.cloned.1.call-done = bf16[8,32,4096]{1,0,2:T(8,128)(2,1)} async-done(((bf16[8,32,64]{1,0,2:T(8,128)(2,1)}), bf16[8,32,4096]{1,0,2:T(8,128)(2,1)}) %all-gather.6.cloned.1.call-update) | async-done | bytes 2097168 | tf_op jit(solution)/shard_map/all_gather | solution.py:43
  117.2 9.4 %copy.43 = bf16[8,32,4096]{2,1,0:T(8,128)(2,1)} copy(bf16[8,32,4096]{1,0,2:T(8,128)(2,1)} %all-gather.6.cloned.1.call-done) | data formatting | bytes 4194304 | tf_op jit(solution)/shard_map/all_gather | solution.py:43
  126.5 80.0 %all-gather.8.cloned.1.call-done = bf16[8,32,4096]{1,0,2:T(8,128)(2,1)} async-done(((bf16[8,32,64]{1,0,2:T(8,128)(2,1)}), bf16[8,32,4096]{1,0,2:T(8,128)(2,1)}) %all-gather.8.cloned.1.call-update) | async-done | bytes 2097168 | tf_op jit(solution)/shard_map/all_gather | solution.py:42
  206.6 9.4 %copy.46 = bf16[8,32,4096]{2,1,0:T(8,128)(2,1)} copy(bf16[8,32,4096]{1,0,2:T(8,128)(2,1)} %all-gather.8.cloned.1.call-done) | data formatting | bytes 4194304 | tf_op jit(solution)/shard_map/all_gather | solution.py:42
  216.0 2.5 fusion.2
  218.7 0.8 fusion.12
  219.5 2.9 fusion
  222.5 67.5 %all-gather.10.cloned.1.call-done = bf16[4096,256]{1,0:T(8,128)(2,1)} async-done(((bf16[64,256]{1,0:T(8,128)(2,1)}), bf16[4096,256]{1,0:T(8,128)(2,1)}) %all-gather.10.cloned.1.call-update) | async-done | bytes 2097168 | tf_op jit(solution)/shard_map/all_gather | solution.py:74
  290.0 3.1 fusion.15
  293.2 1.3 fusion.34
  294.7 144.6 %reduce-scatter.2.cloned.1.call-done = f32[256,64]{0,1:T(8,128)} async-done(((f32[256,4096]{0,1:T(8,128)}), f32[256,64]{0,1:T(8,128)}) %reduce-scatter.2.cloned.1.call-update) | async-done | bytes 65552 | tf_op jit(solution)/shard_map/reduce_scatter | solution.py:58
  439.3 0.8 convert_element_type.37
  441.0 6.5 %all-to-all-start.2 = ((bf16[8,2,1024]{2,1,0:T(2,128)(2,1)}), bf16[8,2,1024]{2,1,0:T(2,128)(2,1)S(1)}, u32[]{:S(2)}, u32[]{:S(2)}) async-start(bf16[8,2,1024]{2,1,0:T(2,128)(2,1)} %reshape.127), calls=%async_computation.3 | async-start | bytes 65536 | tf_op jit(solution)/shard_map/all_to_all | solution.py:61
  447.4 6.9 %all-to-all-done.2 = bf16[8,2,1024]{2,1,0:T(2,128)(2,1)S(1)} async-done(((bf16[8,2,1024]{2,1,0:T(2,128)(2,1)}), bf16[8,2,1024]{2,1,0:T(2,128)(2,1)S(1)}, u32[]{:S(2)}, u32[]{:S(2)}) %all-to-all-start.2) | async-done | bytes 32800 | tf_op jit(solution)/shard_map/all_to_all | solution.py:61
  454.4 0.7 convolution_convert_fusion.2
  455.2 96.9 %all-gather.12.cloned.1.call-done = f32[16384,256]{1,0:T(8,128)} async-done(((f32[256,256]{1,0:T(8,128)}), f32[16384,256]{1,0:T(8,128)}) %all-gather.12.cloned.1.call-update) | async-done | bytes 16777232 | tf_op jit(solution)/shard_map/all_gather | solution.py:83
  552.1 6.8 %reduce_sum.49 = f32[256,256]{1,0:T(8,128)S(1)} reduce(f32[64,256,256]{2,1,0:T(8,128)} %bitcast.84, f32[]{:T(128)} %constant.99.clone.1), dimensions={0}, to_apply=%region_6.7 | reduce | flops 4128768 | bytes 17039364 | tf_op jit(solution)/shard_map/reduce_sum | solution.py:83
  559.3 11.7 %cholesky.50 = f32[128,128]{1,0:T(8,128)S(1)} custom-call(f32[128,128]{1,0:T(8,128)S(1)} %cholesky.118), custom_call_target="Cholesky" | custom-call | tf_op jit(solution)/shard_map/jit(cholesky)/cholesky | solution.py:85
  571.1 0.8 copy.51
  572.0 9.8 %custom-call.18 = f32[1,128,128]{1,2,0:T(8,128)S(1)} custom-call(f32[1,128,128]{2,1,0:T(8,128)S(1)} %get-tuple-element.40), custom_call_target="InvertDiagBlocksLowerTriangular" | custom-call | tf_op jit(solution)/shard_map/jit(cholesky)/cholesky | solution.py:85
  582.2 11.7 %cholesky.105 = f32[128,128]{1,0:T(8,128)S(1)} custom-call(f32[128,128]{1,0:T(8,128)S(1)} %convolution_subtract_fusion.2), custom_call_target="Cholesky" | custom-call | tf_op jit(solution)/shard_map/jit(cholesky)/cholesky | solution.py:85
  596.2 4.1 while.1
  596.8 1.4 bitcast_dynamic-update-slice_fusion.2
  598.8 1.4 bitcast_dynamic-update-slice_fusion.2
  600.3 19.9 %custom-call.19 = f32[2,128,128]{1,2,0:T(8,128)S(1)} custom-call(f32[2,128,128]{2,1,0:T(8,128)S(1)} %get-tuple-element.10), custom_call_target="InvertDiagBlocksLowerTriangular" | custom-call | tf_op jit(solution)/shard_map/jit(_cho_solve)/triangular_solve | solution.py:86
  (66 shorter events, 10.3 us)
Async XLA Ops:
  7.2 208.8 %copy-start = (bf16[1,224,4096]{2,1,0:T(8,128)(2,1)S(1)}, bf16[1,224,4096]{2,1,0:T(8,128)(2,1)}, u32[]{:S(2)}) copy-start(bf16[1,224,4096]{2,1,0:T(8,128)(2,1)} %param.12) | copy-start | bytes 5505028
  7.2 110.0 %all-gather.6.cloned.1.call-start = ((), (), s32[]{:S(2)}) async-start(), calls=%async_computation.4 | async-start | bytes 8519680 | tf_op jit(solution)/shard_map/all_gather | solution.py:43
  26.5 180.0 %all-gather.8.cloned.1.call-start = ((), (), s32[]{:S(2)}) async-start(), calls=%async_computation.5 | async-start | bytes 8519680 | tf_op jit(solution)/shard_map/all_gather | solution.py:42
  37.9 252.1 %all-gather.10.cloned.1.call-start = ((), (), s32[]{:S(2)}) async-start(), calls=%async_computation.7 | async-start | bytes 2129920 | tf_op jit(solution)/shard_map/all_gather | solution.py:74
  38.6 400.6 %reduce-scatter.2.cloned.1.call-start = ((), (), s32[]{:S(2)}) async-start(), calls=%async_computation.6 | async-start | bytes 4259840 | tf_op jit(solution)/shard_map/reduce_scatter | solution.py:58
  216.0 2.5 copy-start.1
  216.0 2.8 copy-start.3
  222.4 72.1 %copy-start.2 = (f32[1,256,256]{2,1,0:T(8,128)S(1)}, f32[1,256,256]{2,1,0:T(8,128)}, u32[]{:S(2)}) copy-start(f32[1,256,256]{2,1,0:T(8,128)} %param.15) | copy-start | bytes 786436
  222.4 329.6 %all-gather.12.cloned.1.call-start = ((), (), s32[]{:S(2)}) async-start(), calls=%async_computation.8 | async-start | bytes 17039360 | tf_op jit(solution)/shard_map/all_gather | solution.py:83
  441.0 13.3 %all-to-all-start.2 = ((bf16[8,2,1024]{2,1,0:T(2,128)(2,1)}), bf16[8,2,1024]{2,1,0:T(2,128)(2,1)S(1)}, u32[]{:S(2)}, u32[]{:S(2)}) async-start(bf16[8,2,1024]{2,1,0:T(2,128)(2,1)} %reshape.127), calls=%async_computation.3 | async-start | bytes 65536 | tf_op jit(solution)/shard_map/all_to_all | solution.py:61
Sparse Core Ops, SparseCore 0:
  26.7 90.4 all-gather.5
  121.1 85.4 all-gather.7
  209.9 80.0 all-gather.9
  294.6 144.6 reduce-scatter.1
  443.0 108.9 all-gather.11
